TPU v7x, 512 devices: a whole 4x8x8 slice. The times are simulated.
512 devices in a mesh: wide: 64 (over y_hi, z, x), narrow: 8 (over y_lo, core).
Axes of the slice: x: 4, y: 8 (y_hi: 2, y_lo: 4; y = y_hi * 4 + y_lo), z: 8, core: 2. Of those that a mesh axis runs over, the one named last changes fastest.
Arguments:
- hidden_in: bfloat16 [16384, 2048], P('wide', 'narrow'), may hold values from -32 to 32
- attn_gain: bfloat16 [2048], P('narrow'), may hold values from 0.099609375 to 1.8984375
- qkv_weight: bfloat16 [2048, 1920], P('narrow', 'wide'), may hold values from -0.125 to 0.125
- q_gain: bfloat16 [64], replicated, may hold values from 1 to 2
- k_gain: bfloat16 [64], replicated, may hold values from 1 to 2
- out_weight: bfloat16 [1280, 2048], P('wide', 'narrow'), may hold values from -0.3125 to 0.3125
- lengths: int32 [4], replicated, may hold values from 1 to 8192, 16384 in all
- page_table: int32 [256], P('wide'), may hold values from 0 to 3, as said below
Outputs:
- hidden_out: bfloat16 [16384, 2048], P('wide', 'narrow')
- kv_cache: bfloat16 [256, 64, 640], P('wide', 'narrow')
Inputs may be any that keep to these rules, and one draw needn't show every extreme that they name: `lengths`: the 4 prompts sum to 16384 tokens and the longest has exactly 8192. `page_table`: each aligned block of 4 entries holds each slot once.
All inputs are finite; a program needn't handle non-finite values.
Results may differ from a plain program's by a relative error of at most 0.0033.
The roundings to bfloat16 on the way count: a program that leaves them out, or rounds other values in their place, can miss the bound.
Values may be sent and summed in bfloat16 or wider, within the bound.
No kernel may reach another device: no remote copies, remote signals or barrier semaphores. Data moves between devices by JAX's collectives and lax.ppermute only.
A program may use at most 128 MiB of HBM per device.

v0:
```python
import math
import jax
import jax.numpy as jnp
from jax import lax
from jax.sharding import PartitionSpec as P

D = 2048
HEADS = 20
KV_HEADS = 5
HEAD = 64
PAGE = 64
GROUP = 4
Q_DIM = 1280
KV_DIM = 640
rope_base = 10000.0


def token_place(token_ids, lengths):
    prompt_ends = jnp.cumsum(lengths)
    prompt_starts = prompt_ends - lengths
    segment = jnp.sum((token_ids[:, None] >= prompt_ends[None, :]).astype(jnp.int32), axis=1)
    matches = segment[:, None] == jnp.arange(lengths.shape[0], dtype=jnp.int32)[None, :]
    position = token_ids - jnp.sum(jnp.where(matches, prompt_starts[None, :], 0), axis=1)
    return (segment, position)


def rotate(projected_part, head_count, head_gain, position):
    row_count = projected_part.shape[0]
    per_head = projected_part.reshape(row_count, head_count, HEAD)
    per_head = per_head * lax.rsqrt(jnp.mean(per_head * per_head, axis=-1, keepdims=True) + 1e-06)
    per_head = per_head * head_gain.astype(jnp.float32)
    halfway = HEAD // 2
    frequency = jnp.exp(
        jnp.arange(halfway, dtype=jnp.float32) * (-2.0 * math.log(rope_base) / HEAD)
    )
    angles = position.astype(jnp.float32)[:, None] * frequency[None, :]
    cosine_table = jnp.cos(angles)[:, None, :]
    sine_table = jnp.sin(angles)[:, None, :]
    lower_half = per_head[..., :halfway]
    upper_half = per_head[..., halfway:]
    rotated = jnp.concatenate(
        [
            lower_half * cosine_table - upper_half * sine_table,
            upper_half * cosine_table + lower_half * sine_table,
        ],
        axis=-1,
    )
    return rotated.reshape(row_count, head_count * HEAD)


def on_device(hidden_in, attn_gain, qkv_weight, q_gain, k_gain, out_weight, lengths, page_table):
    tokens_dev = hidden_in.shape[0]
    narrow_count = lax.axis_size("narrow")
    narrow_index = lax.axis_index("narrow")
    wide_index = lax.axis_index("wide")
    rows_page = PAGE // narrow_count
    pages_dev = tokens_dev // PAGE
    slice_rows = pages_dev * rows_page
    key_width = KV_DIM // 2
    scale = HEAD ** (-0.5)
    input_values = hidden_in.astype(jnp.float32)
    scaled = (input_values * attn_gain.astype(jnp.float32)[None, :]).astype(jnp.bfloat16)
    square_part = jnp.sum(input_values * input_values, axis=1)
    partial_sums = jnp.dot(
        scaled,
        lax.all_gather(qkv_weight, "wide", axis=1, tiled=True),
        preferred_element_type=jnp.float32,
    )
    first_token = wide_index * tokens_dev
    all_tokens = first_token + jnp.arange(tokens_dev, dtype=jnp.int32)
    own_tokens = (
        first_token
        + jnp.arange(pages_dev, dtype=jnp.int32)[:, None] * PAGE
        + narrow_index * rows_page
        + jnp.arange(rows_page, dtype=jnp.int32)[None, :]
    ).reshape(-1)
    segment_all, position_all = token_place(all_tokens, lengths)
    segment_own, position_own = token_place(own_tokens, lengths)
    summed, squares = lax.psum((partial_sums, square_part), "narrow")
    inverse_norm = lax.rsqrt(squares / D + 1e-06)
    projected = summed * inverse_norm[:, None]
    queries = rotate(projected[:, :Q_DIM], HEADS, q_gain, position_all).astype(jnp.bfloat16)
    own_rows = lax.dynamic_index_in_dim(
        projected[:, Q_DIM:].reshape(pages_dev, narrow_count, rows_page, KV_DIM),
        narrow_index,
        1,
        keepdims=False,
    ).reshape(slice_rows, KV_DIM)
    keys_own = rotate(own_rows[:, :key_width], KV_HEADS, k_gain, position_own).astype(jnp.bfloat16)
    values_own = own_rows[:, key_width:].astype(jnp.bfloat16)
    cache_rows = jnp.concatenate([keys_own, values_own], axis=1).reshape(
        pages_dev, rows_page, KV_DIM
    )
    paged_cache = jnp.zeros_like(cache_rows).at[page_table].set(cache_rows)
    query_groups = queries.reshape(tokens_dev, KV_HEADS, GROUP, HEAD)
    key_block = lax.all_gather(keys_own, "wide", axis=0, tiled=True)
    value_block = lax.all_gather(values_own, "wide", axis=0, tiled=True)
    key_count = key_block.shape[0]
    row_index = jnp.arange(key_count, dtype=jnp.int32)
    shard_index = row_index // slice_rows
    inner_index = row_index % slice_rows
    key_tokens = (
        shard_index * tokens_dev
        + inner_index // rows_page * PAGE
        + narrow_index * rows_page
        + inner_index % rows_page
    )
    key_segment, unused = token_place(key_tokens, lengths)
    visible = (key_segment[None, :] == segment_all[:, None]) & (
        key_tokens[None, :] <= all_tokens[:, None]
    )
    scores = (
        jnp.einsum(
            "tkgd,nkd->tkgn",
            query_groups,
            key_block.reshape(key_count, KV_HEADS, HEAD),
            preferred_element_type=jnp.float32,
        )
        * scale
    )
    weights = jnp.where(visible[:, None, None, :], jnp.exp(scores), 0.0)
    numerator = jnp.einsum(
        "tkgn,nkd->tkgd",
        weights.astype(jnp.bfloat16),
        value_block.reshape(key_count, KV_HEADS, HEAD),
        preferred_element_type=jnp.float32,
    )
    denominator = jnp.sum(weights, axis=-1)
    numerator, denominator = (numerator, denominator)
    numerator, denominator = lax.psum((numerator, denominator), "narrow")
    attended = (numerator / denominator[..., None]).reshape(tokens_dev, Q_DIM).astype(jnp.bfloat16)
    mixed_rows = jnp.dot(
        attended,
        lax.all_gather(out_weight, "wide", axis=0, tiled=True),
        preferred_element_type=jnp.float32,
    )
    hidden_out = (input_values + mixed_rows).astype(jnp.bfloat16)
    return (hidden_out, paged_cache)


def solution(mesh):
    return jax.shard_map(
        on_device,
        mesh=mesh,
        in_specs=(
            P("wide", "narrow"),
            P("narrow"),
            P("narrow", "wide"),
            P(),
            P(),
            P("wide", "narrow"),
            P(),
            P("wide"),
        ),
        out_specs=(P("wide", "narrow"), P("wide", "narrow", None)),
        check_vma=False,
    )
```

profile of v0, /device:TPU:32, one launch (start us, length us, event | category | flops | bytes accessed | tf_op | source)
XLA Modules:
  0.0 860.2 jit_solution(7487213716153726544)
XLA Ops:
  7.2 229.6 %all-gather = bf16[64,30,256]{2,1,0:T(8,128)(2,1)S(1)} all-gather(bf16[1,30,256]{2,1,0:T(8,128)(2,1)} %bitcast.51), channel_id=1, replica_groups=mesh['wide'=64,'narrow'=8] {'wide'}, dimensions={0}, use_global_device_ids=true | all-gather | bytes 998400 | tf_op jit(solution)/shard_map/all_gather | solution.py:66
  236.8 0.3 reshape.393
  237.1 1.8 fusion.11
  238.9 0.6 copy-done.8
  240.0 13.7 %psum.29 = f32[256]{0:T(256)S(1)} all-reduce(f32[256]{0:T(256)S(1)} %fusion.10), channel_id=1, replica_groups=mesh['wide'=64,'narrow'=8] {'narrow'}, use_global_device_ids=true, to_apply=%region_2.3 | all-reduce | flops 256 | bytes 2048 | tf_op jit(solution)/shard_map/psum | solution.py:79
  254.1 61.9 %all-reduce.3.cloned.1.call-done = f32[256,1920]{1,0:T(8,128)} async-done(((f32[256,1920]{1,0:T(8,128)}), f32[256,1920]{1,0:T(8,128)}) %all-reduce.3.cloned.1.call-update) | async-done | bytes 1966096 | tf_op jit(solution)/shard_map/psum | solution.py:79
  316.0 1.7 broadcast_multiply_fusion
  318.4 0.7 convert_element_type.68
  319.1 0.5 convert_element_type.69
  320.2 2.3 compare_and_fusion
  322.5 0.7 slice.50
  323.2 0.4 copy.31
  323.9 0.3 multiply_multiply_fusion
  324.4 122.7 %all-gather.7.cloned.1.call-done = bf16[2048,320]{1,0:T(8,128)(2,1)} async-done(((bf16[32,320]{1,0:T(8,128)(2,1)}), bf16[2048,320]{1,0:T(8,128)(2,1)}) %all-gather.7.cloned.1.call-update) | async-done | bytes 1310736 | tf_op jit(solution)/shard_map/all_gather | solution.py:96
  447.1 1.7 copy.30
  448.8 15.7 %fusion = (f32[256,5,4]{0,2,1:T(4,128)S(1)}, f32[5,2048,256,4]{2,1,3,0:T(8,128)}) fusion(pred[256,2048]{0,1:T(8,128)(4,1)S(1)} %copy-done.1, bf16[2048,5,64,1]{0,2,3,1:T(8,128)(2,1)S(1)} %bitcast.46, bf16[256,5,4,64]{0,3,2,1:T(8,128)(2,1)S(1)} %bitcast.49), kind=kOutput, calls=%fused_computation.2 | convolution fusion | flops 1373629440 | bytes 44453888 | tf_op jit(solution)/shard_map/tkgd,nkd->tkgn/dot_general | solution.py:113
  464.5 114.4 %all-gather.5.cloned.1.call-done = bf16[2048,320]{1,0:T(8,128)(2,1)} async-done(((bf16[32,320]{1,0:T(8,128)(2,1)}), bf16[2048,320]{1,0:T(8,128)(2,1)}) %all-gather.5.cloned.1.call-update) | async-done | bytes 1310736 | tf_op jit(solution)/shard_map/all_gather | solution.py:97
  578.9 1.7 copy.29
  580.6 17.4 %fusion.5 = f32[256,5,4,64]{0,3,2,1:T(8,128)} fusion(bf16[2048,5,64,1]{0,2,3,1:T(8,128)(2,1)S(1)} %bitcast.47, f32[5,2048,256,4]{2,1,3,0:T(8,128)} %get-tuple-element.11, pred[256,2048]{0,1:T(8,128)(4,1)S(1)} %copy-done.1), kind=kOutput, calls=%fused_computation.7 | convolution fusion | flops 1373634560 | bytes 45088768 | tf_op jit(solution)/shard_map/tkgn,nkd->tkgd/dot_general | solution.py:122
  598.0 226.0 %all-gather.1 = bf16[64,20,256]{2,1,0:T(8,128)(2,1)S(1)} all-gather(bf16[1,20,256]{2,1,0:T(8,128)(2,1)S(1)} %bitcast.52), channel_id=1, replica_groups=mesh['wide'=64,'narrow'=8] {'wide'}, dimensions={0}, use_global_device_ids=true | all-gather | bytes 665600 | tf_op jit(solution)/shard_map/all_gather | solution.py:134
  824.3 0.6 scatter_fusion
  825.0 26.2 %psum.31 = f32[256,5,4]{0,2,1:T(4,128)S(1)} all-reduce(f32[256,5,4]{0,2,1:T(4,128)S(1)} %get-tuple-element.10), channel_id=1, replica_groups=mesh['wide'=64,'narrow'=8] {'narrow'}, use_global_device_ids=true, to_apply=%region_13.14 | all-reduce | flops 5120 | bytes 40960 | tf_op jit(solution)/shard_map/psum | solution.py:130
  851.2 1.5 divide_convert_fusion
  852.6 1.0 fusion.8
  (71 shorter events, 2.8 us)
Async XLA Ops:
  7.2 229.9 %copy-start.7 = (bf16[256]{0:T(256)(128)(2,1)S(1)}, bf16[256]{0:T(256)(128)(2,1)}, u32[]{:S(2)}) copy-start(bf16[256]{0:T(256)(128)(2,1)} %param.9) | copy-start | bytes 1540
  7.2 229.9 %copy-start = (bf16[256,256]{1,0:T(8,128)(2,1)S(1)}, bf16[256,256]{1,0:T(8,128)(2,1)}, u32[]{:S(2)}) copy-start(bf16[256,256]{1,0:T(8,128)(2,1)} %param.8) | copy-start | bytes 393220
  7.2 308.8 %all-reduce.3.cloned.1.call-start = ((), (), s32[]{:S(2)}) async-start(), calls=%async_computation | async-start | bytes 3932160 | tf_op jit(solution)/shard_map/psum | solution.py:79
  238.9 0.7 copy-start.8
  238.9 0.8 copy-start.9
  238.9 208.2 %all-gather.7.cloned.1.call-start = ((), (), s32[]{:S(2)}) async-start(), calls=%async_computation.2 | async-start | bytes 1597440 | tf_op jit(solution)/shard_map/all_gather | solution.py:96
  317.7 1.4 copy-start.10
  319.1 259.8 %all-gather.5.cloned.1.call-start = ((), (), s32[]{:S(2)}) async-start(), calls=%async_computation.1 | async-start | bytes 1597440 | tf_op jit(solution)/shard_map/all_gather | solution.py:97
  323.2 0.6 copy-start.6
  323.8 527.4 %all-reduce.5.cloned.1.call-start = ((), (), s32[]{:S(2)}) async-start(), calls=%async_computation.3 | async-start | bytes 2621440 | tf_op jit(solution)/shard_map/psum | solution.py:130
  324.4 124.4 %copy-start.1 = (pred[256,2048]{0,1:T(8,128)(4,1)S(1)}, pred[256,2048]{0,1:T(8,128)(4,1)}, u32[]{:S(2)}) copy-start(pred[256,2048]{0,1:T(8,128)(4,1)} %compare_and_fusion) | copy-start | bytes 1572868
  580.5 17.5 %copy-start.5 = (bf16[20,256]{1,0:T(8,128)(2,1)S(1)}, bf16[20,256]{1,0:T(8,128)(2,1)}, u32[]{:S(2)}) copy-start(bf16[20,256]{1,0:T(8,128)(2,1)} %param.13) | copy-start | bytes 30724
  598.0 226.2 %copy-start.11 = (s32[4]{0:T(128)S(1)}, s32[4]{0:T(128)}, u32[]{:S(2)}) copy-start(s32[4]{0:T(128)} %param.15) | copy-start | bytes 52
  598.0 226.2 %copy-start.2 = (bf16[32,320]{1,0:T(8,128)(2,1)S(1)}, bf16[32,320]{1,0:T(8,128)(2,1)}, u32[]{:S(2)}) copy-start(bf16[32,320]{1,0:T(8,128)(2,1)} %slice.50) | copy-start | bytes 61444
  598.0 226.2 %copy-start.3 = (bf16[32,320]{1,0:T(8,128)(2,1)S(1)}, bf16[32,320]{1,0:T(8,128)(2,1)}, u32[]{:S(2)}) copy-start(bf16[32,320]{1,0:T(8,128)(2,1)} %convert_element_type.68) | copy-start | bytes 61444
  825.0 28.7 %copy-start.4 = (bf16[4,8,640]{2,1,0:T(8,128)(2,1)}, bf16[4,8,640]{2,1,0:T(8,128)(2,1)S(1)}, u32[]{:S(2)}) copy-start(bf16[4,8,640]{2,1,0:T(8,128)(2,1)S(1)} %scatter_fusion) | copy-start | bytes 122884
Sparse Core Ops, SparseCore 0:
  239.0 76.9 all-reduce.2
  321.9 125.1 all-gather.6
  453.1 125.7 all-gather.4
  598.1 81.6 all-reduce.4
where the time goes:
time: 861 us; the launch traced here: 860 us
  blocking collectives  496 us (58%)
  waiting for transfers between devices  299 us (35%)
  matrix products  35.9 us (4%)
  between operations  14.1 us (2%)
    all_gather x1, blocking collectives, on_device(): lax.all_gather(qkv_weight, 'wide', axis=1, tiled=True)  230 us
    all_gather x1, blocking collectives, on_device(): lax.all_gather(out_weight, 'wide', axis=0, tiled=True)  226 us
    all_gather x1, waiting for transfers between devices, on_device(): key_block = lax.all_gather(keys_own, 'wide', axis=0, tiled=True)  123 us
    all_gather x1, waiting for transfers between devices, on_device(): value_block = lax.all_gather(values_own, 'wide', axis=0, tiled=True)  114 us
    psum x1, waiting for transfers between devices, on_device(): summed, squares = lax.psum((partial_sums, square_part), 'narrow')  61.9 us
    psum x1, blocking collectives, on_device(): numerator, denominator = lax.psum((numerator, denominator), 'narrow')  26.2 us
    dot_general x1, matrix products, on_device(): jnp.einsum('tkgn,nkd->tkgd', weights.astype(jnp.bfloat16), value_block.re...  17.4 us
  transfers between devices with their start and end apart: 4, of which 3 were waited for; matrix products, arithmetic and copies ran while one was open for 3% of the time, Pallas kernels for 0%

commit v1 on v0

--- a/solution.py
+++ b/solution.py
@@ -94,7 +94,9 @@
     paged_cache = jnp.zeros_like(cache_rows).at[page_table].set(cache_rows)
     query_groups = queries.reshape(tokens_dev, KV_HEADS, GROUP, HEAD)
     key_block = lax.all_gather(keys_own, "wide", axis=0, tiled=True)
-    value_block = lax.all_gather(values_own, "wide", axis=0, tiled=True)
+    value_block = jnp.concatenate(
+        lax.all_to_all(jnp.stack([values_own] * lax.axis_size("wide")), "wide", 0, 0), axis=0
+    )
     key_count = key_block.shape[0]
     row_index = jnp.arange(key_count, dtype=jnp.int32)
     shard_index = row_index // slice_rows

time: 861 us -> 769 us (0.89)
  waiting for transfers between devices: 299 us -> 187 us
  starting transfers between devices: 0.16 us -> 15.9 us
    all_gather x1 -> x0, waiting for transfers between devices: 114 us -> none  [on_device(): value_block = lax.all_gather(values_own, 'wide', axis=0, tiled=True)]
    all_to_all x0 -> x1, starting transfers between devices: none -> 15.8 us  [on_device(): lax.all_to_all(jnp.stack([values_own] * lax.axis_size('wide')), 'wide', 0...]
  transfers between devices with their start and end apart: 4 -> 4, of which waited for: 3 -> 2; matrix products, arithmetic and copies ran while one was open for 3% -> 3% of each run, Pallas kernels for 0% -> 0%
where the time goes in v1:
time: 769 us
  blocking collectives  496 us (64%)
  waiting for transfers between devices  187 us (24%)
  matrix products  38.8 us (5%)
  starting transfers between devices  15.9 us (2%)
  between operations  14.1 us (2%)
  local copies, waits for them, and re-layouts  8.76 us (1%)
  other arithmetic  7.83 us (1%)
    all_gather x1, blocking collectives, on_device(): lax.all_gather(qkv_weight, 'wide', axis=1, tiled=True)  230 us
    all_gather x1, blocking collectives, on_device(): lax.all_gather(out_weight, 'wide', axis=0, tiled=True)  226 us
    all_gather x1, waiting for transfers between devices, on_device(): key_block = lax.all_gather(keys_own, 'wide', axis=0, tiled=True)  125 us
    psum x1, waiting for transfers between devices, on_device(): summed, squares = lax.psum((partial_sums, square_part), 'narrow')  62.5 us
    psum x1, blocking collectives, on_device(): numerator, denominator = lax.psum((numerator, denominator), 'narrow')  26.7 us
    dot_general x1, matrix products, on_device(): jnp.einsum('tkgn,nkd->tkgd', weights.astype(jnp.bfloat16), value_block.re...  18.9 us
    dot_general x1, matrix products, on_device(): jnp.einsum('tkgd,nkd->tkgn', query_groups, key_block.reshape(key_count, K...  17.2 us
    all_to_all x1, starting transfers between devices, on_device(): lax.all_to_all(jnp.stack([values_own] * lax.axis_size('wide')), 'wide', 0...  15.8 us
  transfers between devices with their start and end apart: 4, of which 2 were waited for; matrix products, arithmetic and copies ran while one was open for 3% of the time, Pallas kernels for 0%

profile of v1, /device:TPU:32, one launch (start us, length us, event | category | flops | bytes accessed | tf_op | source)
XLA Modules:
  0.0 768.8 jit_solution(4996524667803514727)
XLA Ops:
  7.2 229.6 %all-gather = bf16[64,30,256]{2,1,0:T(8,128)(2,1)S(1)} all-gather(bf16[1,30,256]{2,1,0:T(8,128)(2,1)} %bitcast.46), channel_id=1, replica_groups=mesh['wide'=64,'narrow'=8] {'wide'}, dimensions={0}, use_global_device_ids=true | all-gather | bytes 998400 | tf_op jit(solution)/shard_map/all_gather | solution.py:66
  236.8 0.3 reshape.391
  237.1 1.8 fusion.14
  239.5 13.8 %psum.29 = f32[256]{0:T(256)S(1)} all-reduce(f32[256]{0:T(256)S(1)} %fusion.13), channel_id=1, replica_groups=mesh['wide'=64,'narrow'=8] {'narrow'}, use_global_device_ids=true, to_apply=%region_2.3 | all-reduce | flops 256 | bytes 2048 | tf_op jit(solution)/shard_map/psum | solution.py:79
  253.6 62.5 %all-reduce.3.cloned.1.call-done = f32[256,1920]{1,0:T(8,128)} async-done(((f32[256,1920]{1,0:T(8,128)}), f32[256,1920]{1,0:T(8,128)}) %all-reduce.3.cloned.1.call-update) | async-done | bytes 1966096 | tf_op jit(solution)/shard_map/psum | solution.py:79
  316.1 1.7 broadcast_multiply_fusion
  318.5 0.7 convert_element_type.68
  319.5 0.2 multiply_cosine_fusion
  319.7 2.3 compare_and_fusion
  322.2 0.4 copy.30
  322.6 1.3 stack.2
  323.9 15.8 %all-to-all-start = ((bf16[64,32,320]{2,1,0:T(8,128)(2,1)}), bf16[64,32,320]{2,1,0:T(8,128)(2,1)S(1)}, u32[]{:S(2)}, u32[]{:S(2)}) async-start(bf16[64,32,320]{2,1,0:T(8,128)(2,1)} %stack.2), calls=%async_computation | async-start | bytes 3145728 | tf_op jit(solution)/shard_map/all_to_all | solution.py:98
  339.9 0.3 multiply_multiply_fusion
  340.2 0.2 subtract_convert_fusion
  340.4 124.5 %all-gather.4.cloned.1.call-done = bf16[2048,320]{1,0:T(8,128)(2,1)} async-done(((bf16[32,320]{1,0:T(8,128)(2,1)}), bf16[2048,320]{1,0:T(8,128)(2,1)}) %all-gather.4.cloned.1.call-update) | async-done | bytes 1310736 | tf_op jit(solution)/shard_map/all_gather | solution.py:96
  464.9 1.7 copy.29
  466.6 17.2 %fusion = (f32[256,5,4]{0,2,1:T(4,128)}, f32[5,2048,256,4]{2,1,3,0:T(8,128)}) fusion(pred[256,2048]{0,1:T(8,128)(4,1)} %compare_and_fusion, bf16[2048,5,64,1]{0,2,3,1:T(8,128)(2,1)S(1)} %bitcast.42, bf16[256,5,4,64]{0,3,2,1:T(8,128)(2,1)S(1)} %bitcast.44), kind=kOutput, calls=%fused_computation.2 | convolution fusion | flops 1373629440 | bytes 44453888 | tf_op jit(solution)/shard_map/tkgd,nkd->tkgn/dot_general | solution.py:115
  483.8 3.2 reshape_reshape.3
  487.0 18.9 %fusion.6 = f32[256,5,4,64]{0,3,2,1:T(8,128)} fusion(f32[5,2048,256,4]{2,1,3,0:T(8,128)} %get-tuple-element.11, pred[256,2048]{0,1:T(8,128)(4,1)S(1)} %copy-done.2, bf16[2048,5,64,1]{2,1,0,3:T(8,128)(2,1)} %bitcast.41), kind=kOutput, calls=%fused_computation.8 | convolution fusion | flops 1373634560 | bytes 45088768 | tf_op jit(solution)/shard_map/tkgn,nkd->tkgd/dot_general | solution.py:124
  505.9 226.2 %all-gather.1 = bf16[64,20,256]{2,1,0:T(8,128)(2,1)S(1)} all-gather(bf16[1,20,256]{2,1,0:T(8,128)(2,1)S(1)} %bitcast.47), channel_id=1, replica_groups=mesh['wide'=64,'narrow'=8] {'wide'}, dimensions={0}, use_global_device_ids=true | all-gather | bytes 665600 | tf_op jit(solution)/shard_map/all_gather | solution.py:136
  732.4 0.6 scatter_fusion
  733.0 26.7 %psum.31 = f32[256,5,4]{0,2,1:T(4,128)S(1)} all-reduce(f32[256,5,4]{0,2,1:T(4,128)S(1)} %copy-done.7), channel_id=1, replica_groups=mesh['wide'=64,'narrow'=8] {'narrow'}, use_global_device_ids=true, to_apply=%region_13.14 | all-reduce | flops 5120 | bytes 40960 | tf_op jit(solution)/shard_map/psum | solution.py:132
  759.7 1.5 divide_convert_fusion
  761.2 1.0 fusion.11
  (75 shorter events, 2.5 us)
Async XLA Ops:
  7.2 229.9 %copy-start.9 = (bf16[256]{0:T(256)(128)(2,1)S(1)}, bf16[256]{0:T(256)(128)(2,1)}, u32[]{:S(2)}) copy-start(bf16[256]{0:T(256)(128)(2,1)} %param.9) | copy-start | bytes 1540
  7.2 229.9 %copy-start = (bf16[256,256]{1,0:T(8,128)(2,1)S(1)}, bf16[256,256]{1,0:T(8,128)(2,1)}, u32[]{:S(2)}) copy-start(bf16[256,256]{1,0:T(8,128)(2,1)} %param.8) | copy-start | bytes 393220
  7.2 308.9 %all-reduce.3.cloned.1.call-start = ((), (), s32[]{:S(2)}) async-start(), calls=%async_computation.1 | async-start | bytes 3932160 | tf_op jit(solution)/shard_map/psum | solution.py:79
  237.1 1.9 copy-start.10
  237.1 2.0 copy-start.11
  238.9 226.0 %all-gather.4.cloned.1.call-start = ((), (), s32[]{:S(2)}) async-start(), calls=%async_computation.2 | async-start | bytes 1597440 | tf_op jit(solution)/shard_map/all_gather | solution.py:96
  317.8 1.4 copy-start.12
  322.2 1.7 copy-start.4
  323.9 160.0 %all-to-all-start = ((bf16[64,32,320]{2,1,0:T(8,128)(2,1)}), bf16[64,32,320]{2,1,0:T(8,128)(2,1)S(1)}, u32[]{:S(2)}, u32[]{:S(2)}) async-start(bf16[64,32,320]{2,1,0:T(8,128)(2,1)} %stack.2), calls=%async_computation | async-start | bytes 3145728 | tf_op jit(solution)/shard_map/all_to_all | solution.py:98
  339.7 420.1 %all-reduce.5.cloned.1.call-start = ((), (), s32[]{:S(2)}) async-start(), calls=%async_computation.3 | async-start | bytes 2621440 | tf_op jit(solution)/shard_map/psum | solution.py:132
  483.8 3.2 copy-start.2
  487.0 18.9 %copy-start.8 = (bf16[20,256]{1,0:T(8,128)(2,1)S(1)}, bf16[20,256]{1,0:T(8,128)(2,1)}, u32[]{:S(2)}) copy-start(bf16[20,256]{1,0:T(8,128)(2,1)} %param.13) | copy-start | bytes 30724
  505.8 226.4 %copy-start.13 = (s32[4]{0:T(128)S(1)}, s32[4]{0:T(128)}, u32[]{:S(2)}) copy-start(s32[4]{0:T(128)} %param.15) | copy-start | bytes 52
  505.8 226.4 %copy-start.3 = (bf16[32,320]{1,0:T(8,128)(2,1)S(1)}, bf16[32,320]{1,0:T(8,128)(2,1)}, u32[]{:S(2)}) copy-start(bf16[32,320]{1,0:T(8,128)(2,1)} %convert_element_type.68) | copy-start | bytes 61444
  505.9 226.4 %copy-start.5 = (bf16[32,320]{1,0:T(8,128)(2,1)S(1)}, bf16[32,320]{1,0:T(8,128)(2,1)}, u32[]{:S(2)}) copy-start(bf16[32,320]{1,0:T(8,128)(2,1)} %copy-done.4) | copy-start | bytes 61444
  505.9 227.2 %copy-start.7 = (f32[256,5,4]{0,2,1:T(4,128)S(1)}, f32[256,5,4]{0,2,1:T(4,128)}, u32[]{:S(2)}) copy-start(f32[256,5,4]{0,2,1:T(4,128)} %get-tuple-element.10) | copy-start | bytes 61444
  732.1 29.1 %copy-start.1 = (bf16[256,256]{1,0:T(8,128)(2,1)S(1)}, bf16[256,256]{1,0:T(8,128)(2,1)}, u32[]{:S(2)}) copy-start(bf16[256,256]{1,0:T(8,128)(2,1)} %param.8) | copy-start | bytes 393220
  733.0 29.3 %copy-start.6 = (bf16[4,8,640]{2,1,0:T(8,128)(2,1)}, bf16[4,8,640]{2,1,0:T(8,128)(2,1)S(1)}, u32[]{:S(2)}) copy-start(bf16[4,8,640]{2,1,0:T(8,128)(2,1)S(1)} %scatter_fusion) | copy-start | bytes 122884
Sparse Core Ops, SparseCore 0:
  239.0 77.0 all-reduce.2
  322.0 142.8 all-gather.3
  506.0 81.5 all-reduce.4
